TPU v7x, 512 devices: a whole 4x4x16 slice. The times are simulated.
512 devices in a mesh: rep: 8 (over y, core), exp: 64 (over x, z).
Axes of the slice: x: 4, y: 4, z: 16, core: 2. Of those that a mesh axis runs over, the one named last changes fastest.
Arguments:
- payload: bfloat16 [16384, 2048], P(('rep', 'exp')), may hold values from -6 to 6
- block_scales: bfloat16 [16384, 16], P(('rep', 'exp')), may hold values from 0.29882812 to 3
- cotangent: bfloat16 [16384, 2048], P(('rep', 'exp')), may hold values from -12 to 12
- expert_ids: int32 [16384, 8], P(('rep', 'exp')), may hold values from 0 to 63, all different within a row; in each aligned block of 32 rows (0 to 31, 32 to 63, ...) at most 5 rows name the same one
- route_counts: int32 [16384, 8], P(('rep', 'exp')), may hold values from 1 to 15
- gate_up: bfloat16 [64, 2, 2048, 384], P('exp', None, 'rep'), may hold values from -0.125 to 0.125
- down_weight: bfloat16 [64, 384, 2048], P('exp', None, 'rep'), may hold values from -0.3125 to 0.3125
- first_moment: float32 [64, 2, 2048, 384], P('exp', None, 'rep'), may hold values from -12 to 12
- second_moment: float32 [64, 2, 2048, 384], P('exp', None, 'rep'), may hold values from 10 to 300
Outputs:
- d_activation: bfloat16 [16384, 2048], P(('rep', 'exp'))
- new_first: float32 [64, 2, 2048, 384], P('exp', None, 'rep')
- new_second: float32 [64, 2, 2048, 384], P('exp', None, 'rep')
- weight_step: bfloat16 [64, 2, 2048, 384], P('exp', None, 'rep')
Inputs may be any that keep to these rules, and one draw needn't show every extreme that they name: `expert_ids`: in the rows of one device (aligned blocks of 32 tokens) no expert is named more than 5 times, a bound that some block reaches; each token names 8 different experts.
All inputs are finite; a program needn't handle non-finite values.
Results may differ from a plain program's by a relative error of at most 0.02.
Values may be sent and summed in bfloat16 or wider, within the bound.
A program may use at most 64 MiB of HBM per device.

v0:
```python
import jax
import jax.numpy as jnp
import numpy as np
from jax import lax
from jax.sharding import PartitionSpec as P

X_SIZE = 4
Z_SIZE = 16
CAPACITY = 5
Z_GROUPS = [[x * Z_SIZE + z for z in range(Z_SIZE)] for x in range(X_SIZE)]
X_GROUPS = [[x * Z_SIZE + z for x in range(X_SIZE)] for z in range(Z_SIZE)]


def silu_parts(gate_pre):
    sigmoid_val = jax.nn.sigmoid(gate_pre)
    return (gate_pre * sigmoid_val, sigmoid_val * (1.0 + gate_pre * (1.0 - sigmoid_val)))


def dequantize(values, scales):
    array_shape = values.shape
    blocked = values.astype(jnp.float32).reshape(
        array_shape[:-1] + (scales.shape[-1], array_shape[-1] // scales.shape[-1])
    )
    return (
        (blocked * scales.astype(jnp.float32)[..., None]).reshape(array_shape).astype(jnp.bfloat16)
    )


def route_tables(ids, counts, z_pos, tok_rows):
    count_float = counts.astype(jnp.float32)
    share = count_float / jnp.sum(count_float, axis=1, keepdims=True)
    experts = jnp.arange(X_SIZE, dtype=jnp.int32) * Z_SIZE + z_pos
    hit = ids[None] == experts[:, None, None]
    match = jnp.any(hit, axis=2)
    weight = jnp.sum(jnp.where(hit, share[None], 0.0), axis=2)
    ones = match.astype(jnp.bfloat16).reshape(X_SIZE * Z_SIZE, tok_rows)
    before = jnp.asarray(np.triu(np.ones((tok_rows, tok_rows)), 1), jnp.bfloat16)
    rank = jnp.dot(ones, before, preferred_element_type=jnp.float32).astype(jnp.int32)
    base = jnp.arange(Z_SIZE, dtype=jnp.int32)[None, :, None] * CAPACITY
    slot = (base + rank.reshape(X_SIZE, Z_SIZE, tok_rows)).reshape(X_SIZE, Z_SIZE * tok_rows)
    slot = jnp.where(match, slot, -1)
    lanes = jnp.arange(Z_SIZE * CAPACITY, dtype=jnp.int32)
    pick = slot[:, None, :] == lanes[None, :, None]
    slot_share = jnp.sum(jnp.where(pick, weight[:, None, :], 0.0), axis=2)
    pick = pick.reshape(X_SIZE * Z_SIZE * CAPACITY, Z_SIZE * tok_rows).astype(jnp.bfloat16)
    return (pick, slot_share.reshape(X_SIZE * Z_SIZE * CAPACITY))


def on_device(
    payload,
    block_scales,
    cotangent,
    expert_ids,
    route_counts,
    gate_up,
    down_weight,
    first_moment,
    second_moment,
):
    tok_rows, width = payload.shape
    replicas = lax.axis_size("rep")
    z_pos = lax.axis_index("exp") % Z_SIZE
    side = Z_SIZE * CAPACITY
    slot_count = X_SIZE * side
    activation = dequantize(payload, block_scales)
    routing = jnp.concatenate([expert_ids, route_counts], axis=1).astype(jnp.bfloat16)
    routing = jnp.pad(routing, ((0, 0), (0, 112)))
    act_all = lax.all_gather(
        jnp.concatenate([activation, routing], axis=1),
        "exp",
        axis=0,
        tiled=True,
        axis_index_groups=Z_GROUPS,
    )
    cot_all = lax.all_gather(cotangent, "exp", axis=0, tiled=True, axis_index_groups=Z_GROUPS)
    whole_gate_up = lax.all_gather(gate_up, "rep", axis=2, tiled=True)
    whole_down = lax.all_gather(down_weight, "rep", axis=2, tiled=True)
    top = expert_ids.shape[1]
    ids = act_all[:, width : width + top].astype(jnp.int32)
    counts = act_all[:, width + top : width + 2 * top].astype(jnp.int32)
    pick, slot_share = route_tables(ids, counts, z_pos, tok_rows)

    def to_experts(rows):
        return lax.all_to_all(
            rows.reshape(X_SIZE, side, width),
            "exp",
            split_axis=0,
            concat_axis=0,
            tiled=True,
            axis_index_groups=X_GROUPS,
        )

    act_rows = jnp.dot(pick, act_all[:, :width], preferred_element_type=jnp.float32)
    input_rows = to_experts(act_rows.astype(jnp.bfloat16)).reshape(slot_count, width)
    cot_rows = jnp.dot(pick, cot_all, preferred_element_type=jnp.float32)
    cot_rows = (slot_share[:, None] * cot_rows).astype(jnp.bfloat16)
    cotan_rows = to_experts(cot_rows).reshape(slot_count, width)
    pre_acts = jnp.einsum(
        "sd,tdf->tsf", input_rows, whole_gate_up[0], preferred_element_type=jnp.float32
    )
    hidden_grad = jnp.einsum(
        "sd,fd->sf", cotan_rows, whole_down[0], preferred_element_type=jnp.float32
    )
    silu_val, silu_slope = silu_parts(pre_acts[0])
    gate_grad = (hidden_grad * pre_acts[1] * silu_slope).astype(jnp.bfloat16)
    up_grad = (hidden_grad * silu_val).astype(jnp.bfloat16)
    row_grad = (
        jnp.einsum("sf,df->sd", gate_grad, whole_gate_up[0, 0], preferred_element_type=jnp.float32)
        + jnp.einsum("sf,df->sd", up_grad, whole_gate_up[0, 1], preferred_element_type=jnp.float32)
    ).astype(jnp.bfloat16)
    home = to_experts(row_grad).reshape(slot_count, width)
    partial = jnp.einsum("st,sd->td", pick, home, preferred_element_type=jnp.float32)
    d_activation = lax.psum_scatter(
        partial.astype(jnp.bfloat16),
        "exp",
        scatter_dimension=0,
        tiled=True,
        axis_index_groups=Z_GROUPS,
    )
    hidden_width = gate_grad.shape[1]
    both_grads = jnp.concatenate([gate_grad, up_grad], axis=1)
    term = jnp.einsum("sd,sf->df", input_rows, both_grads, preferred_element_type=jnp.float32)
    term = lax.optimization_barrier(term.astype(jnp.bfloat16))
    local_square = jnp.sum(jnp.square(term.astype(jnp.float32)))
    summed = lax.psum_scatter(term, "rep", scatter_dimension=0, tiled=True).astype(jnp.float32)
    shard_rows = width // replicas
    grad_shard = summed.reshape(shard_rows, 2, hidden_width).transpose(1, 0, 2)
    small_sum, big_sum = lax.psum((local_square, jnp.sum(jnp.square(grad_shard))), "rep")
    entry_count = 2.0 * width * hidden_width
    small_norm = small_sum / (replicas * entry_count)
    big_norm = big_sum / (replicas * replicas * entry_count)
    noise_gain = replicas * big_norm / (small_norm + 1e-06)
    new_first = 0.9 * first_moment + 0.1 * grad_shard[None]
    new_second = 0.95 * second_moment + 0.05 * jnp.square(grad_shard[None])
    weight_step = (noise_gain * new_first / (jnp.sqrt(new_second) + 1e-08)).astype(jnp.bfloat16)
    return (d_activation, new_first, new_second, weight_step)


def solution(mesh):
    tokens = P(("rep", "exp"), None)
    shards = P("exp", None, "rep", None)
    return jax.shard_map(
        on_device,
        mesh=mesh,
        in_specs=(tokens,) * 5 + (shards, P("exp", None, "rep"), shards, shards),
        out_specs=(tokens, shards, shards, shards),
        check_vma=False,
    )
```

profile of v0, /device:TPU:6, one launch (start us, length us, event | category | flops | bytes accessed | tf_op | source)
XLA Modules:
  0.0 364.9 jit_solution(17802854460447803655)
XLA Ops:
  9.7 1.0 fusion.22
  13.8 75.3 %all-gather.5.cloned.1.call-done = bf16[512,2176]{1,0:T(8,128)(2,1)} async-done(((bf16[32,2176]{1,0:T(8,128)(2,1)}), bf16[512,2176]{1,0:T(8,128)(2,1)}) %all-gather.5.cloned.1.call-update) | async-done | bytes 2228240 | tf_op jit(solution)/shard_map/all_gather | solution.py:68
  89.0 1.1 fusion.30
  91.0 3.5 convolution_convert_fusion.1
  94.5 4.8 %all-to-all-start.1 = ((bf16[4,80,2048]{2,1,0:T(8,128)(2,1)}), bf16[4,80,2048]{2,1,0:T(8,128)(2,1)S(1)}, u32[]{:S(2)}, u32[]{:S(2)}) async-start(bf16[4,80,2048]{2,1,0:T(8,128)(2,1)} %bitcast.4), calls=%async_computation.1 | async-start | bytes 2621440 | tf_op jit(solution)/shard_map/all_to_all | solution.py:84
  99.7 61.3 %all-gather.7.cloned.1.call-done = bf16[512,2048]{1,0:T(8,128)(2,1)} async-done(((bf16[32,2048]{1,0:T(8,128)(2,1)}), bf16[512,2048]{1,0:T(8,128)(2,1)}) %all-gather.7.cloned.1.call-update) | async-done | bytes 2097168 | tf_op jit(solution)/shard_map/all_gather | solution.py:75
  161.0 3.5 fusion.3
  164.5 4.8 %all-to-all-start = ((bf16[4,80,2048]{2,1,0:T(8,128)(2,1)}), bf16[4,80,2048]{2,1,0:T(8,128)(2,1)S(1)}, u32[]{:S(2)}, u32[]{:S(2)}) async-start(bf16[4,80,2048]{2,1,0:T(8,128)(2,1)} %bitcast.1), calls=%async_computation | async-start | bytes 2621440 | tf_op jit(solution)/shard_map/all_to_all | solution.py:84
  169.3 26.2 %all-gather.11.cloned.1.call-done = bf16[1,2,2048,384]{3,2,1,0:T(8,128)(2,1)} async-done(((bf16[1,2,256,384]{3,2,1,0:T(8,128)(2,1)}), bf16[1,2,2048,384]{3,2,1,0:T(8,128)(2,1)}) %all-gather.11.cloned.1.call-update) | async-done | bytes 3145744 | tf_op jit(solution)/shard_map/all_gather | solution.py:76
  195.5 4.0 %fusion.8 = f32[2,320,384]{2,1,0:T(8,128)} fusion(bf16[320,2048,1]{1,0,2:T(8,128)(2,1)S(1)} %bitcast.88, bf16[1,2,2048,384]{3,2,1,0:T(8,128)(2,1)} %all-gather.11.cloned.1.call-done), kind=kOutput, calls=%fused_computation.16 | convolution fusion | flops 1006632960 | bytes 5439488 | tf_op jit(solution)/shard_map/sd,tdf->tsf/dot_general | solution.py:98
  199.5 30.6 %all-gather.9.cloned.1.call-done = bf16[1,384,2048]{2,1,0:T(8,128)(2,1)} async-done(((bf16[1,384,256]{2,1,0:T(8,128)(2,1)}), bf16[1,384,2048]{2,1,0:T(8,128)(2,1)}) %all-gather.9.cloned.1.call-update) | async-done | bytes 1572880 | tf_op jit(solution)/shard_map/all_gather | solution.py:77
  230.1 2.6 multiply_convert_fusion
  233.4 3.5 convolution_convert_fusion
  237.0 1.8 copy-done.1
  238.8 0.9 fusion.5
  239.7 0.9 fusion.2
  240.6 20.8 %all_to_all.15 = bf16[4,80,2048]{2,1,0:T(8,128)(2,1)S(1)} all-to-all(bf16[4,80,2048]{2,1,0:T(8,128)(2,1)S(1)} %bitcast.85), channel_id=1, replica_groups={{0,16,32,48},{1,17,33,49},{2,18,34,50},{3,19,35,51},{4,20,36,52},{5,21,..., dimensions={0} | all-to-all | bytes 2621440 | tf_op jit(solution)/shard_map/all_to_all | solution.py:84
  261.5 2.7 bitcast_convert_fusion
  264.1 2.2 multiply_reduce_fusion
  266.4 15.5 %reduce-scatter.5.cloned.1.call-done = bf16[256,768]{1,0:T(8,128)(2,1)} async-done(((bf16[2048,768]{1,0:T(8,128)(2,1)}), bf16[256,768]{1,0:T(8,128)(2,1)}) %reduce-scatter.5.cloned.1.call-update) | async-done | bytes 393232 | tf_op jit(solution)/shard_map/reduce_scatter | solution.py:125
  281.8 1.8 convert_multiply_fusion.1
  283.6 13.5 %all-reduce.1 = (f32[]{:T(128)}, f32[]{:T(128)}) all-reduce(f32[]{:T(128)} %get-tuple-element.14, f32[]{:T(128)} %multiply_reduce_fusion), channel_id=1, replica_groups=mesh['rep'=8,'exp'=64] {'rep'}, use_global_device_ids=true, to_apply=%region_7.8 | all-reduce | flops 2 | bytes 16 | tf_op jit(solution)/shard_map/psum | solution.py:128
  298.5 1.4 divide_convert_fusion
  300.0 58.1 %reduce-scatter.3.cloned.1.call-done = bf16[32,2048]{1,0:T(8,128)(2,1)} async-done(((bf16[512,2048]{1,0:T(8,128)(2,1)}), bf16[32,2048]{1,0:T(8,128)(2,1)}) %reduce-scatter.3.cloned.1.call-update) | async-done | bytes 131088 | tf_op jit(solution)/shard_map/reduce_scatter | solution.py:113
  (56 shorter events, 7.6 us)
Async XLA Ops:
  7.2 83.3 %copy-start.6 = (bf16[32,32]{1,0:T(8,128)(2,1)S(1)}, bf16[32,32]{1,0:T(8,128)(2,1)}, u32[]{:S(2)}) copy-start(bf16[32,32]{1,0:T(8,128)(2,1)} %constant.52.clone) | copy-start | bytes 6148
  7.2 81.9 %all-gather.5.cloned.1.call-start = ((), (), s32[]{:S(2)}) async-start(), calls=%async_computation.5 | async-start | bytes 2367488 | tf_op jit(solution)/shard_map/all_gather | solution.py:68
  11.4 149.6 %all-gather.7.cloned.1.call-start = ((), (), s32[]{:S(2)}) async-start(), calls=%async_computation.6 | async-start | bytes 2228224 | tf_op jit(solution)/shard_map/all_gather | solution.py:75
  12.2 183.3 %all-gather.11.cloned.1.call-start = ((), (), s32[]{:S(2)}) async-start(), calls=%async_computation.8 | async-start | bytes 3538944 | tf_op jit(solution)/shard_map/all_gather | solution.py:76
  12.9 217.2 %all-gather.9.cloned.1.call-start = ((), (), s32[]{:S(2)}) async-start(), calls=%async_computation.7 | async-start | bytes 1769472 | tf_op jit(solution)/shard_map/all_gather | solution.py:77
  94.5 70.1 %all-to-all-start.1 = ((bf16[4,80,2048]{2,1,0:T(8,128)(2,1)}), bf16[4,80,2048]{2,1,0:T(8,128)(2,1)S(1)}, u32[]{:S(2)}, u32[]{:S(2)}) async-start(bf16[4,80,2048]{2,1,0:T(8,128)(2,1)} %bitcast.4), calls=%async_computation.1 | async-start | bytes 2621440 | tf_op jit(solution)/shard_map/all_to_all | solution.py:84
  164.5 65.6 %all-to-all-start = ((bf16[4,80,2048]{2,1,0:T(8,128)(2,1)}), bf16[4,80,2048]{2,1,0:T(8,128)(2,1)S(1)}, u32[]{:S(2)}, u32[]{:S(2)}) async-start(bf16[4,80,2048]{2,1,0:T(8,128)(2,1)} %bitcast.1), calls=%async_computation | async-start | bytes 2621440 | tf_op jit(solution)/shard_map/all_to_all | solution.py:84
  169.3 112.5 %reduce-scatter.5.cloned.1.call-start = ((), (), s32[]{:S(2)}) async-start(), calls=%async_computation.10 | async-start | bytes 3538944 | tf_op jit(solution)/shard_map/reduce_scatter | solution.py:125
  232.7 0.7 copy-start.4
  236.9 1.9 copy-start.1
  236.9 121.2 %reduce-scatter.3.cloned.1.call-start = ((), (), s32[]{:S(2)}) async-start(), calls=%async_computation.9 | async-start | bytes 2228224 | tf_op jit(solution)/shard_map/reduce_scatter | solution.py:113
  238.8 0.9 copy-start.5
  261.5 2.7 copy-start
  266.4 32.1 %copy-start.2 = (f32[1,2,256,384]{3,2,1,0:T(8,128)S(1)}, f32[1,2,256,384]{3,2,1,0:T(8,128)}, u32[]{:S(2)}) copy-start(f32[1,2,256,384]{3,2,1,0:T(8,128)} %param.18) | copy-start | bytes 2359300
  266.4 32.1 %copy-start.3 = (f32[1,2,256,384]{3,2,1,0:T(8,128)S(1)}, f32[1,2,256,384]{3,2,1,0:T(8,128)}, u32[]{:S(2)}) copy-start(f32[1,2,256,384]{3,2,1,0:T(8,128)} %param.17) | copy-start | bytes 2359300
Sparse Core Ops, SparseCore 0:
  11.6 77.4 all-gather.4
  91.1 69.8 all-gather.6
  163.2 32.2 all-gather.10
  197.4 32.5 all-gather.8
  237.0 44.7 reduce-scatter.4
  285.1 72.9 reduce-scatter.2
where the time goes:
time: 366 us; the launch traced here: 365 us
  waiting for transfers between devices  269 us (73%)
  blocking collectives  34.4 us (9%)
  matrix products  21.7 us (6%)
  between operations  15.6 us (4%)
  starting transfers between devices  9.77 us (3%)
  other arithmetic  7.83 us (2%)
  local copies, waits for them, and re-layouts  6.8 us (2%)
    all_gather x1, waiting for transfers between devices, on_device(): lax.all_gather(jnp.concatenate([activation, routing], axis=1), 'exp', axi...  75.3 us
    all_gather x1, waiting for transfers between devices, on_device(): lax.all_gather(cotangent, 'exp', axis=0, tiled=True, axis_index_groups=Z_...  61.3 us
    reduce_scatter x1, waiting for transfers between devices, on_device(): lax.psum_scatter(partial.astype(jnp.bfloat16), 'exp', scatter_dimension=0...  58.1 us
    all_gather x1, waiting for transfers between devices, on_device(): whole_down = lax.all_gather(down_weight, 'rep', axis=2, tiled=True)  30.6 us
    all_gather x1, waiting for transfers between devices, on_device(): whole_gate_up = lax.all_gather(gate_up, 'rep', axis=2, tiled=True)  26.2 us
    all_to_all x1, blocking collectives, to_experts(): lax.all_to_all(rows.reshape(X_SIZE, side, width), 'exp', split_axis=0, co...  20.8 us
    reduce_scatter x1, waiting for transfers between devices, on_device(): lax.psum_scatter(term, 'rep', scatter_dimension=0, tiled=True)  15.5 us
    psum x1, blocking collectives, on_device(): lax.psum((local_square, jnp.sum(jnp.square(grad_shard))), 'rep')  13.5 us
  transfers between devices with their start and end apart: 8, of which 6 were waited for; matrix products, arithmetic and copies ran while one was open for 6% of the time, Pallas kernels for 0%

commit v1 on v0

--- a/solution.py
+++ b/solution.py
@@ -74,7 +74,9 @@
     )
     cot_all = lax.all_gather(cotangent, "exp", axis=0, tiled=True, axis_index_groups=Z_GROUPS)
     whole_gate_up = lax.all_gather(gate_up, "rep", axis=2, tiled=True)
-    whole_down = lax.all_gather(down_weight, "rep", axis=2, tiled=True)
+    whole_down = jnp.concatenate(
+        lax.all_to_all(jnp.stack([down_weight] * lax.axis_size("rep")), "rep", 0, 0), axis=2
+    )
     top = expert_ids.shape[1]
     ids = act_all[:, width : width + top].astype(jnp.int32)
     counts = act_all[:, width + top : width + 2 * top].astype(jnp.int32)

time: 366 us -> 334 us (0.913)
  waiting for transfers between devices: 269 us -> 230 us
  starting transfers between devices: 9.77 us -> 14.3 us
    all_gather x1 -> x0, waiting for transfers between devices: 30.6 us -> none  [on_device(): whole_down = lax.all_gather(down_weight, 'rep', axis=2, tiled=True)]
    all_gather x1, waiting for transfers between devices: 75.3 us -> 68.9 us  [on_device(): lax.all_gather(jnp.concatenate([activation, routing], axis=1), 'exp', axi...]
    all_to_all x0 -> x1, starting transfers between devices: none -> 4.6 us  [on_device(): lax.all_to_all(jnp.stack([down_weight] * lax.axis_size('rep')), 'rep', 0, 0)]
  transfers between devices with their start and end apart: 8 -> 8, of which waited for: 6 -> 5; matrix products, arithmetic and copies ran while one was open for 6% -> 8% of each run, Pallas kernels for 0% -> 0%
where the time goes in v1:
time: 334 us; the launch traced here: 333 us
  waiting for transfers between devices  230 us (69%)
  blocking collectives  34.3 us (10%)
  matrix products  21.8 us (7%)
  between operations  15.2 us (5%)
  starting transfers between devices  14.3 us (4%)
  local copies, waits for them, and re-layouts  9.27 us (3%)
  other arithmetic  7.83 us (2%)
    all_gather x1, waiting for transfers between devices, on_device(): lax.all_gather(jnp.concatenate([activation, routing], axis=1), 'exp', axi...  68.9 us
    all_gather x1, waiting for transfers between devices, on_device(): lax.all_gather(cotangent, 'exp', axis=0, tiled=True, axis_index_groups=Z_...  61.1 us
    reduce_scatter x1, waiting for transfers between devices, on_device(): lax.psum_scatter(partial.astype(jnp.bfloat16), 'exp', scatter_dimension=0...  58 us
    all_gather x1, waiting for transfers between devices, on_device(): whole_gate_up = lax.all_gather(gate_up, 'rep', axis=2, tiled=True)  26 us
    all_to_all x1, blocking collectives, to_experts(): lax.all_to_all(rows.reshape(X_SIZE, side, width), 'exp', split_axis=0, co...  20.8 us
    reduce_scatter x1, waiting for transfers between devices, on_device(): lax.psum_scatter(term, 'rep', scatter_dimension=0, tiled=True)  14.5 us
    psum x1, blocking collectives, on_device(): lax.psum((local_square, jnp.sum(jnp.square(grad_shard))), 'rep')  13.5 us
    all_to_all x2, starting transfers between devices, to_experts(): lax.all_to_all(rows.reshape(X_SIZE, side, width), 'exp', split_axis=0, co...  9.58 us
  transfers between devices with their start and end apart: 8, of which 5 were waited for; matrix products, arithmetic and copies ran while one was open for 8% of the time, Pallas kernels for 0%

profile of v1, /device:TPU:6, one launch (start us, length us, event | category | flops | bytes accessed | tf_op | source)
XLA Modules:
  0.0 332.8 jit_solution(13560788651903672731)
XLA Ops:
  9.7 1.0 fusion.20
  12.9 1.1 copy.52
  14.0 1.4 stack.2
  15.4 4.6 %all-to-all-start.1 = ((bf16[8,1,384,256]{2,3,1,0:T(8,128)(2,1)}), bf16[8,1,384,256]{2,3,1,0:T(8,128)(2,1)S(1)}, u32[]{:S(2)}, u32[]{:S(2)}) async-start(bf16[8,1,384,256]{2,3,1,0:T(8,128)(2,1)} %stack.2), calls=%async_computation.1 | async-start | bytes 3145728 | tf_op jit(solution)/shard_map/all_to_all | solution.py:78
  20.2 68.9 %all-gather.4.cloned.1.call-done = bf16[512,2176]{1,0:T(8,128)(2,1)} async-done(((bf16[32,2176]{1,0:T(8,128)(2,1)}), bf16[512,2176]{1,0:T(8,128)(2,1)}) %all-gather.4.cloned.1.call-update) | async-done | bytes 2228240 | tf_op jit(solution)/shard_map/all_gather | solution.py:68
  89.1 1.1 fusion.28
  91.0 3.5 %convolution_convert_fusion.1 = bf16[320,2048]{1,0:T(8,128)(2,1)} fusion(pred[320,512]{1,0:T(32,128)(4,1)S(1)} %bitcast_compare_fusion, bf16[512,2176]{1,0:T(8,128)(2,1)} %all-gather.4.cloned.1.call-done), kind=kOutput, calls=%fused_computation.9 | convolution fusion | flops 671744000 | bytes 3571712 | tf_op jit(solution)/shard_map/dot_general | solution.py:95
  94.5 4.8 %all-to-all-start.2 = ((bf16[4,80,2048]{2,1,0:T(8,128)(2,1)}), bf16[4,80,2048]{2,1,0:T(8,128)(2,1)S(1)}, u32[]{:S(2)}, u32[]{:S(2)}) async-start(bf16[4,80,2048]{2,1,0:T(8,128)(2,1)} %bitcast.93), calls=%async_computation.2 | async-start | bytes 2621440 | tf_op jit(solution)/shard_map/all_to_all | solution.py:86
  99.8 61.1 %all-gather.6.cloned.1.call-done = bf16[512,2048]{1,0:T(8,128)(2,1)} async-done(((bf16[32,2048]{1,0:T(8,128)(2,1)}), bf16[512,2048]{1,0:T(8,128)(2,1)}) %all-gather.6.cloned.1.call-update) | async-done | bytes 2097168 | tf_op jit(solution)/shard_map/all_gather | solution.py:75
  160.9 3.6 %fusion.3 = bf16[320,2048]{1,0:T(8,128)(2,1)} fusion(pred[320,512]{1,0:T(32,128)(4,1)S(1)} %bitcast_compare_fusion, bf16[512,2048]{1,0:T(8,128)(2,1)} %all-gather.6.cloned.1.call-done, f32[320]{0:T(512)S(1)} %mul.107), kind=kOutput, calls=%fused_computation.8 | convolution fusion | flops 672399360 | bytes 3572992 | tf_op jit(solution)/shard_map/dot_general | solution.py:97
  164.5 4.8 %all-to-all-start = ((bf16[4,80,2048]{2,1,0:T(8,128)(2,1)}), bf16[4,80,2048]{2,1,0:T(8,128)(2,1)}, u32[]{:S(2)}, u32[]{:S(2)}) async-start(bf16[4,80,2048]{2,1,0:T(8,128)(2,1)} %bitcast.94), calls=%async_computation | async-start | bytes 2621440 | tf_op jit(solution)/shard_map/all_to_all | solution.py:86
  169.3 26.0 %all-gather.8.cloned.1.call-done = bf16[1,2,2048,384]{3,2,1,0:T(8,128)(2,1)} async-done(((bf16[1,2,256,384]{3,2,1,0:T(8,128)(2,1)}), bf16[1,2,2048,384]{3,2,1,0:T(8,128)(2,1)}) %all-gather.8.cloned.1.call-update) | async-done | bytes 3145744 | tf_op jit(solution)/shard_map/all_gather | solution.py:76
  195.4 4.0 %fusion.6 = f32[2,320,384]{2,1,0:T(8,128)} fusion(bf16[320,2048,1]{1,0,2:T(8,128)(2,1)S(1)} %bitcast.91, bf16[1,2,2048,384]{3,2,1,0:T(8,128)(2,1)} %all-gather.8.cloned.1.call-done), kind=kOutput, calls=%fused_computation.14 | convolution fusion | flops 1006632960 | bytes 5439488 | tf_op jit(solution)/shard_map/sd,tdf->tsf/dot_general | solution.py:100
  199.4 2.5 multiply_convert_fusion
  202.6 3.5 %convolution_convert_fusion = bf16[2048,768]{1,0:T(8,128)(2,1)} fusion(bf16[320,2048]{1,0:T(8,128)(2,1)S(1)} %bitcast.92, bf16[320,384]{1,0:T(8,128)(2,1)S(1)} %get-tuple-element.11, bf16[320,384]{1,0:T(8,128)(2,1)S(1)} %get-tuple-element.12), kind=kOutput, calls=%fused_computation.2 | convolution fusion | flops 1009188864 | bytes 4947968 | tf_op jit(solution)/shard_map/sd,sf->df/dot_general | solution.py:124
  206.2 1.8 copy-done.1
  209.9 20.8 %all_to_all.20 = bf16[4,80,2048]{2,1,0:T(8,128)(2,1)S(1)} all-to-all(bf16[4,80,2048]{2,1,0:T(8,128)(2,1)S(1)} %bitcast.87), channel_id=1, replica_groups={{0,16,32,48},{1,17,33,49},{2,18,34,50},{3,19,35,51},{4,20,36,52},{5,21,..., dimensions={0} | all-to-all | bytes 2621440 | tf_op jit(solution)/shard_map/all_to_all | solution.py:86
  230.7 2.7 bitcast_convert_fusion
  233.4 2.2 multiply_reduce_fusion
  235.6 14.5 %reduce-scatter.5.cloned.1.call-done = bf16[256,768]{1,0:T(8,128)(2,1)} async-done(((bf16[2048,768]{1,0:T(8,128)(2,1)}), bf16[256,768]{1,0:T(8,128)(2,1)}) %reduce-scatter.5.cloned.1.call-update) | async-done | bytes 393232 | tf_op jit(solution)/shard_map/reduce_scatter | solution.py:127
  250.1 1.8 convert_multiply_fusion.1
  251.9 13.5 %all-reduce.1 = (f32[]{:T(128)}, f32[]{:T(128)}) all-reduce(f32[]{:T(128)} %get-tuple-element.14, f32[]{:T(128)} %multiply_reduce_fusion), channel_id=1, replica_groups=mesh['rep'=8,'exp'=64] {'rep'}, use_global_device_ids=true, to_apply=%region_7.8 | all-reduce | flops 2 | bytes 16 | tf_op jit(solution)/shard_map/psum | solution.py:130
  266.8 1.4 divide_convert_fusion
  268.3 58.0 %reduce-scatter.3.cloned.1.call-done = bf16[32,2048]{1,0:T(8,128)(2,1)} async-done(((bf16[512,2048]{1,0:T(8,128)(2,1)}), bf16[32,2048]{1,0:T(8,128)(2,1)}) %reduce-scatter.3.cloned.1.call-update) | async-done | bytes 131088 | tf_op jit(solution)/shard_map/reduce_scatter | solution.py:115
  (57 shorter events, 8.8 us)
Async XLA Ops:
  7.2 81.9 %all-gather.4.cloned.1.call-start = ((), (), s32[]{:S(2)}) async-start(), calls=%async_computation.6 | async-start | bytes 2367488 | tf_op jit(solution)/shard_map/all_gather | solution.py:68
  11.4 149.5 %all-gather.6.cloned.1.call-start = ((), (), s32[]{:S(2)}) async-start(), calls=%async_computation.7 | async-start | bytes 2228224 | tf_op jit(solution)/shard_map/all_gather | solution.py:75
  12.2 183.2 %all-gather.8.cloned.1.call-start = ((), (), s32[]{:S(2)}) async-start(), calls=%async_computation.8 | async-start | bytes 3538944 | tf_op jit(solution)/shard_map/all_gather | solution.py:76
  15.4 75.1 %copy-start.6 = (bf16[32,32]{1,0:T(8,128)(2,1)S(1)}, bf16[32,32]{1,0:T(8,128)(2,1)}, u32[]{:S(2)}) copy-start(bf16[32,32]{1,0:T(8,128)(2,1)} %constant.52.clone) | copy-start | bytes 6148
  15.4 79.2 %all-to-all-start.1 = ((bf16[8,1,384,256]{2,3,1,0:T(8,128)(2,1)}), bf16[8,1,384,256]{2,3,1,0:T(8,128)(2,1)S(1)}, u32[]{:S(2)}, u32[]{:S(2)}) async-start(bf16[8,1,384,256]{2,3,1,0:T(8,128)(2,1)} %stack.2), calls=%async_computation.1 | async-start | bytes 3145728 | tf_op jit(solution)/shard_map/all_to_all | solution.py:78
  94.5 70.0 %all-to-all-start.2 = ((bf16[4,80,2048]{2,1,0:T(8,128)(2,1)}), bf16[4,80,2048]{2,1,0:T(8,128)(2,1)S(1)}, u32[]{:S(2)}, u32[]{:S(2)}) async-start(bf16[4,80,2048]{2,1,0:T(8,128)(2,1)} %bitcast.93), calls=%async_computation.2 | async-start | bytes 2621440 | tf_op jit(solution)/shard_map/all_to_all | solution.py:86
  164.5 34.9 %all-to-all-start = ((bf16[4,80,2048]{2,1,0:T(8,128)(2,1)}), bf16[4,80,2048]{2,1,0:T(8,128)(2,1)}, u32[]{:S(2)}, u32[]{:S(2)}) async-start(bf16[4,80,2048]{2,1,0:T(8,128)(2,1)} %bitcast.94), calls=%async_computation | async-start | bytes 2621440 | tf_op jit(solution)/shard_map/all_to_all | solution.py:86
  169.3 80.8 %reduce-scatter.5.cloned.1.call-start = ((), (), s32[]{:S(2)}) async-start(), calls=%async_computation.10 | async-start | bytes 3538944 | tf_op jit(solution)/shard_map/reduce_scatter | solution.py:127
  201.9 0.7 copy-start.4
  206.1 1.9 copy-start.1
  206.2 120.1 %reduce-scatter.3.cloned.1.call-start = ((), (), s32[]{:S(2)}) async-start(), calls=%async_computation.9 | async-start | bytes 2228224 | tf_op jit(solution)/shard_map/reduce_scatter | solution.py:115
  208.0 0.9 copy-start.5
  230.7 2.7 copy-start
  235.6 31.2 %copy-start.2 = (f32[1,2,256,384]{3,2,1,0:T(8,128)S(1)}, f32[1,2,256,384]{3,2,1,0:T(8,128)}, u32[]{:S(2)}) copy-start(f32[1,2,256,384]{3,2,1,0:T(8,128)} %param.18) | copy-start | bytes 2359300
  235.6 31.2 %copy-start.3 = (f32[1,2,256,384]{3,2,1,0:T(8,128)S(1)}, f32[1,2,256,384]{3,2,1,0:T(8,128)}, u32[]{:S(2)}) copy-start(f32[1,2,256,384]{3,2,1,0:T(8,128)} %param.17) | copy-start | bytes 2359300
Sparse Core Ops, SparseCore 0:
  11.5 77.5 all-gather.3
  91.2 69.6 all-gather.5
  163.1 32.2 all-gather.7
  206.3 43.8 reduce-scatter.4
  253.4 72.8 reduce-scatter.2
